TPU v7x, 256 devices: a whole 4x4x8 slice. The times are simulated.
256 devices in a mesh: band: 8 (over z_lo, core), span: 32 (over x, y, z_hi).
Axes of the slice: x: 4, y: 4, z: 8 (z_hi: 2, z_lo: 4; z = z_hi * 4 + z_lo), core: 2. Of those that a mesh axis runs over, the one named last changes fastest.
Arguments:
- gases: bfloat16 [7, 32, 131072], P(None, None, ('band', 'span')), may hold values from 0 to 1
- pressure_bin: int32 [32, 131072], P(None, ('band', 'span')), may hold values from 0 to 59
- layer_mass: bfloat16 [32, 131072], P(None, ('band', 'span')), may hold values from 0.5 to 2
- cos_zenith: bfloat16 [131072], P(('band', 'span')), may hold values from 0.19921875 to 1
- surface_albedo: bfloat16 [131072], P(('band', 'span')), may hold values from 0.049804688 to 0.8984375
- column_order: int32 [131072], P(('band', 'span')), may hold values from 0 to 511, as said below
- sunlit: int32 [1024], P(('band', 'span')), may hold values from 0 to 1, as said below
- absorption: bfloat16 [112, 7, 60], replicated, may hold values from 9.9658966e-05 to 0.099609375
- scattering: bfloat16 [112, 60], replicated, may hold values from 0.19921875 to 0.94921875
Outputs:
- heating: float32 [32, 131072], P(None, ('band', 'span'))
Inputs may be any that keep to these rules, and one draw needn't show every extreme that they name: `column_order`: the 512 entries of each device's slice are a permutation of 0 to 511. The 8 devices with the same index along the second mesh axis hold 16 sunlit blocks together; among them one device has all 4 blocks sunlit and one has none.
All inputs are finite; a program needn't handle non-finite values.
Results may differ from a plain program's by a relative error of at most 0.0003.
Values may be sent and summed in bfloat16 or wider, within the bound.
A program may use at most 64 MiB of HBM per device.

v0:
```python
import jax
import jax.numpy as jnp
from jax import lax
from jax.sharding import PartitionSpec as P


def column_heating(profile, ground_pair, absorption, scattering):
    gas_count = absorption.shape[1]
    bin_count = scattering.shape[1]
    levels = profile.shape[1]
    col_count = profile.shape[2]
    groups = levels // 8
    amounts = profile[:gas_count]
    bin_index = profile[gas_count].astype(jnp.int32)
    thickness = profile[gas_count + 1].astype(jnp.float32)
    cosine = ground_pair[0, 0].astype(jnp.float32)
    ground = ground_pair[1, 0].astype(jnp.float32)
    selector = (
        bin_index[None] == lax.broadcasted_iota(jnp.int32, (bin_count, levels, col_count), 0)
    ).astype(jnp.bfloat16)
    weighted = (amounts[:, None] * selector[None]).reshape(gas_count * bin_count, levels, col_count)
    table = absorption.reshape(absorption.shape[0], gas_count * bin_count)
    optical_depth = jnp.einsum("gk,kln->lgn", table, weighted, preferred_element_type=jnp.float32)
    albedo = jnp.einsum("gk,kln->lgn", scattering, selector, preferred_element_type=jnp.float32)
    column_path = jnp.cumsum(optical_depth, axis=0)
    column_path = jnp.concatenate([jnp.zeros_like(column_path[:1]), column_path], axis=0)
    direct = cosine * jnp.exp(-column_path / cosine)
    fading = jnp.exp(-1.66 * optical_depth)
    reflect = 0.5 * albedo * (1.0 - fading)
    transmit = fading + reflect
    source = 0.5 * albedo * (direct[:-1] - direct[1:])
    grouped_shape = (groups, 8) + reflect.shape[1:]

    def upward(state_pair, layer):
        refl_below, source_below = state_pair
        layer_reflect, layer_transmit, layer_source = layer
        refl_rows = []
        source_rows = []
        for offset in range(7, -1, -1):
            denominator = 1.0 - layer_reflect[offset] * refl_below
            refl_next = (
                layer_reflect[offset]
                + layer_transmit[offset] * layer_transmit[offset] * refl_below / denominator
            )
            source_below = (
                layer_source[offset]
                + layer_transmit[offset]
                * (source_below + refl_below * layer_source[offset])
                / denominator
            )
            refl_below = refl_next
            refl_rows.insert(0, refl_below)
            source_rows.insert(0, source_below)
        return ((refl_below, source_below), (jnp.stack(refl_rows), jnp.stack(source_rows)))

    floor_refl = jnp.broadcast_to(ground, reflect.shape[1:])
    floor_source = ground * direct[-1]
    final_pair, tops = lax.scan(
        upward,
        (floor_refl, floor_source),
        (
            reflect.reshape(grouped_shape),
            transmit.reshape(grouped_shape),
            source.reshape(grouped_shape),
        ),
        reverse=True,
    )
    refl_all = jnp.concatenate([tops[0].reshape(reflect.shape), floor_refl[None]], axis=0)
    source_all = jnp.concatenate([tops[1].reshape(reflect.shape), floor_source[None]], axis=0)

    def downward(diffuse, layer):
        layer_reflect, layer_transmit, layer_source, refl_low, source_low = layer
        level_rows = []
        for offset in range(8):
            denominator = 1.0 - layer_reflect[offset] * refl_low[offset]
            diffuse = (
                layer_transmit[offset] * diffuse
                + layer_reflect[offset] * source_low[offset]
                + layer_source[offset]
            ) / denominator
            level_rows.append(diffuse)
        return (diffuse, jnp.stack(level_rows))

    start_diffuse = jnp.zeros_like(floor_refl)
    final_diffuse, lower = lax.scan(
        downward,
        start_diffuse,
        (
            reflect.reshape(grouped_shape),
            transmit.reshape(grouped_shape),
            source.reshape(grouped_shape),
            refl_all[1:].reshape(grouped_shape),
            source_all[1:].reshape(grouped_shape),
        ),
    )
    diffuse_all = jnp.concatenate([start_diffuse[None], lower.reshape(reflect.shape)], axis=0)
    net = direct + diffuse_all - (refl_all * diffuse_all + source_all)
    return jnp.sum(net[:-1] - net[1:], axis=1) / thickness


def blocks_heating(field_blocks, ground_blocks, absorption, scattering):
    moved_fields = jnp.moveaxis(field_blocks, 2, 0)
    moved_ground = jnp.moveaxis(ground_blocks, 2, 0)
    result = lax.map(
        lambda inputs_pair: column_heating(inputs_pair[0], inputs_pair[1], absorption, scattering),
        (moved_fields, moved_ground),
    )
    return jnp.moveaxis(result, 0, 1)


def local(
    gases,
    pressure_bin,
    layer_mass,
    cos_zenith,
    surface_albedo,
    column_order,
    sunlit,
    absorption,
    scattering,
):
    band_count = lax.axis_size("band")
    group_size = lax.axis_size("span")
    me_band = lax.axis_index("band")
    columns = column_order.shape[0]
    per_peer = columns // group_size
    block_count = sunlit.shape[0]
    block_cols = columns // block_count
    levels = layer_mass.shape[0]
    fields = jnp.concatenate(
        [gases, pressure_bin.astype(jnp.bfloat16)[None], layer_mass[None]], axis=0
    )
    field_rows = fields.shape[0]
    ground = jnp.stack([cos_zenith, surface_albedo])[:, None]
    ordering = column_order.reshape(group_size, per_peer)
    fields = jnp.take(fields, ordering, axis=2)
    ground = jnp.take(ground, ordering, axis=2)
    fields, ground = (
        lax.all_to_all(fields, "span", split_axis=2, concat_axis=2, tiled=True),
        lax.all_to_all(ground, "span", split_axis=2, concat_axis=2, tiled=True),
    )
    fields = fields.reshape(field_rows, levels, block_count, block_cols)
    ground = ground.reshape(2, 1, block_count, block_cols)
    flag_mask = sunlit.astype(jnp.float32)[:, None]
    flag_table = lax.all_gather(sunlit, "band", axis=0, tiled=True).reshape(band_count, block_count)
    counts = jnp.sum(flag_table, axis=1)
    band_ends = jnp.cumsum(counts)
    starts = band_ends - counts
    own_start = starts[me_band]
    own_rank = jnp.cumsum(sunlit) - sunlit
    slot_count = -(-block_count // band_count)
    working = block_count // 2
    target = jnp.arange(band_count, dtype=jnp.int32)[:, None]
    position = jnp.arange(slot_count, dtype=jnp.int32)[None, :]
    wanted = position * band_count + (target - own_start) % band_count
    matches = (sunlit[None, None, :] == 1) & (own_rank[None, None, :] == wanted[:, :, None])
    chosen = jnp.sum(
        jnp.where(matches, jnp.arange(block_count, dtype=jnp.int32), 0), axis=2
    ).reshape(-1)
    send_fields = jnp.take(fields, chosen, axis=2).reshape(
        field_rows, levels, band_count, slot_count, block_cols
    )
    send_ground = jnp.take(ground, chosen, axis=2).reshape(2, 1, band_count, slot_count, block_cols)
    got_fields, got_ground = (
        lax.all_to_all(send_fields, "band", split_axis=2, concat_axis=2, tiled=True),
        lax.all_to_all(send_ground, "band", split_axis=2, concat_axis=2, tiled=True),
    )
    work_rank = jnp.arange(working, dtype=jnp.int32) * band_count + me_band
    source_band = jnp.sum((band_ends[None, :] <= work_rank[:, None]).astype(jnp.int32), axis=1)
    within = work_rank - starts[source_band]
    work_pick = source_band * slot_count + within // band_count
    work_fields = jnp.take(
        got_fields.reshape(field_rows, levels, band_count * slot_count, block_cols),
        work_pick,
        axis=2,
    )
    work_ground = jnp.take(
        got_ground.reshape(2, 1, band_count * slot_count, block_cols), work_pick, axis=2
    )
    heating = blocks_heating(work_fields, work_ground, absorption, scattering)
    inner_back = position * band_count + (me_band - starts[:, None]) % band_count
    rank_back = starts[:, None] + inner_back
    slot_back = jnp.clip(rank_back // band_count, 0, working - 1).reshape(-1)
    returned = jnp.take(heating, slot_back, axis=1).reshape(
        levels, band_count, slot_count, block_cols
    )
    home_heat = lax.all_to_all(returned, "band", split_axis=1, concat_axis=1, tiled=True)
    dest_back = (own_start + own_rank) % band_count
    spot_index = dest_back * slot_count + own_rank // band_count
    physics_heat = (
        jnp.take(home_heat.reshape(levels, band_count * slot_count, block_cols), spot_index, axis=1)
        * flag_mask
    )
    physics_heat = physics_heat.reshape(levels, group_size, per_peer)
    dyn_heat = lax.all_to_all(
        physics_heat, "span", split_axis=1, concat_axis=1, tiled=True
    ).reshape(levels, columns)
    return jnp.zeros((levels, columns), jnp.float32).at[:, column_order].set(dyn_heat)


def solution(mesh):
    placed = (
        P(None, None, ("band", "span")),
        P(None, ("band", "span")),
        P(None, ("band", "span")),
        P(("band", "span")),
        P(("band", "span")),
        P(("band", "span")),
        P(("band", "span")),
        P(),
        P(),
    )
    return jax.shard_map(
        local, mesh=mesh, in_specs=placed, out_specs=P(None, ("band", "span")), check_vma=False
    )
```

profile of v0, /device:TPU:1, one launch (start us, length us, event | category | flops | bytes accessed | tf_op | source)
XLA Modules:
  0.0 282.3 jit_solution(17097676135511918596)
XLA Ops:
  3.2 1.3 gather_fusion.1
  5.5 14.5 %all-to-all-start = ((bf16[2,1,32,16]{3,0,1,2:T(2,128)(2,1)}), bf16[2,1,32,16]{3,0,1,2:T(2,128)(2,1)S(1)}, u32[]{:S(2)}, u32[]{:S(2)}) async-start(bf16[2,1,32,16]{3,0,1,2:T(2,128)(2,1)} %broadcast_select_fusion.1), calls=%async_computation | async-start | bytes 32768 | tf_op jit(solution)/shard_map/all_to_all | solution.py:140
  22.8 6.8 %all-reduce.2 = s32[32]{0:T(128)S(1)} all-reduce(s32[32]{0:T(128)S(1)} %dynamic-update-slice), channel_id=1, replica_groups=mesh['band'=8,'span'=32] {'band'}, use_global_device_ids=true, to_apply=%add.2 | all-reduce | flops 32 | bytes 256
  32.7 1.9 compare_and_fusion.4
  36.5 2.0 copy.76
  38.5 2.7 gather_fusion.4
  41.2 1.9 copy.77
  43.6 1.5 reshape.960
  45.1 11.3 %all-to-all-start.2 = ((bf16[32,2,2304]{2,1,0:T(2,128)(2,1)}), bf16[32,2,2304]{2,1,0:T(2,128)(2,1)S(1)}, u32[]{:S(2)}, u32[]{:S(2)}) async-start(bf16[32,2,2304]{2,1,0:T(2,128)(2,1)} %reshape.960), calls=%async_computation.2 | async-start | bytes 589824 | tf_op jit(solution)/shard_map/all_to_all | solution.py:139
  58.5 10.5 %all-to-all-done.2 = bf16[32,2,2304]{2,1,0:T(2,128)(2,1)S(1)} async-done(((bf16[32,2,2304]{2,1,0:T(2,128)(2,1)}), bf16[32,2,2304]{2,1,0:T(2,128)(2,1)S(1)}, u32[]{:S(2)}, u32[]{:S(2)}) %all-to-all-start.2) | async-done | bytes 294944 | tf_op jit(solution)/shard_map/all_to_all | solution.py:139
  69.0 7.7 %all-to-all-start.1 = ((bf16[2,1,8,1,128]{4,0,3,1,2:T(2,128)(2,1)}), bf16[2,1,8,1,128]{4,0,3,1,2:T(2,128)(2,1)S(1)}, u32[]{:S(2)}, u32[]{:S(2)}) async-start(bf16[2,1,8,1,128]{4,0,3,1,2:T(2,128)(2,1)} %fusion.84), calls=%async_computation.1 | async-start | bytes 8192 | tf_op jit(solution)/shard_map/all_to_all | solution.py:166
  79.6 1.9 all-to-all-done.1
  81.5 4.1 %all-to-all-start.3 = ((bf16[9,32,8,1,128]{4,1,0,3,2:T(8,128)(2,1)}), bf16[9,32,8,1,128]{4,1,0,3,2:T(8,128)(2,1)S(1)}, u32[]{:S(2)}, u32[]{:S(2)}) async-start(bf16[9,32,8,1,128]{4,1,0,3,2:T(8,128)(2,1)} %fusion.81), calls=%async_computation.3 | async-start | bytes 1179648 | tf_op jit(solution)/shard_map/all_to_all | solution.py:165
  86.4 15.1 %all-to-all-done.3 = bf16[9,32,8,1,128]{4,1,0,3,2:T(8,128)(2,1)S(1)} async-done(((bf16[9,32,8,1,128]{4,1,0,3,2:T(8,128)(2,1)}), bf16[9,32,8,1,128]{4,1,0,3,2:T(8,128)(2,1)S(1)}, u32[]{:S(2)}, u32[]{:S(2)}) %all-to-all-start.3) | async-done | bytes 589856 | tf_op jit(solution)/shard_map/all_to_all | solution.py:165
  102.2 148.1 %while.85 = (s32[]{:T(128)}, f32[2,32,128]{2,1,0:T(8,128)S(1)}, bf16[2,2,1,128]{3,0,1,2:T(2,128)(2,1)S(1)}, bf16[2,9,32,128]{3,2,1,0:T(8,128)(2,1)S(1)}, bf16[11...) while((s32[]{:T(128)}, f32[2,32,128]{2,1,0:T(8,128)S(1)}, ...), condition=%wide.region_12.13_spmd, body=%wide.region_5.12_spmd.sunk | while | flops 469948672 | bytes 88375600 | solution.py:104
  103.2 5.9 %fusion.127 = f32[32,112,128]{2,1,0:T(8,128)S(1)} fusion(f32[32,128,112,1]{1,2,3,0:T(8,128)S(1)} %fusion.126), kind=kOutput, calls=%fused_computation.191.clone.1 | output fusion | flops 14221312 | bytes 3670016 | tf_op jit(solution)/shard_map/while/body/eval_jaxpr/jit(cumsum)/reduce_window_sum | solution.py:25
  110.4 2.8 bitcast_multiply_fusion.5
  113.2 1.4 broadcast.891.clone
  114.6 1.4 broadcast.891.clone.1
  116.0 14.0 %while.86 = (s32[]{:T(128)}, f32[112,128]{1,0:T(8,128)S(1)}, f32[112,128]{1,0:T(8,128)S(1)}, f32[4,8,112,128]{3,2,1,0:T(8,128)}, f32[4,8,112,128]{3,2,1,0:T(8,12...) while((s32[]{:T(128)}, f32[112,128]{1,0:T(8,128)S(1)}, ...), condition=%wide.region_8.8_spmd, body=%wide.region_7.7_spmd.sunk | while | flops 1290248 | bytes 6136109 | solution.py:58
  116.0 1.4 bitcast_dynamic-update-slice_fusion.53
  119.5 1.4 bitcast_dynamic-update-slice_fusion.53
  123.0 1.4 bitcast_dynamic-update-slice_fusion.53
  126.5 1.4 bitcast_dynamic-update-slice_fusion.53
  130.0 3.5 %fusion.131 = f32[32,112,128]{2,1,0:T(8,128)} fusion(f32[1,112,128]{2,1,0:T(8,128)S(1)} %broadcast_in_dim.228, f32[32,112,128]{2,1,0:T(8,128)} %bitcast.650), kind=kLoop, calls=%fused_computation.184.clone.1 | loop fusion | flops 458752 | bytes 3727360 | tf_op jit(solution)/shard_map/while/body/eval_jaxpr/concatenate | solution.py:68
  134.3 2.9 %fusion.130 = f32[32,112,128]{2,1,0:T(8,128)} fusion(f32[1,112,128]{2,1,0:T(8,128)S(1)} %slice_multiply_fusion.2, f32[32,112,128]{2,1,0:T(8,128)} %bitcast.648), kind=kLoop, calls=%fused_computation.183.clone.1 | loop fusion | flops 458752 | bytes 3727360 | tf_op jit(solution)/shard_map/while/body/eval_jaxpr/concatenate | solution.py:69
  137.1 1.4 broadcast.891
  138.5 34.4 %while.87 = (s32[]{:T(128)}, f32[112,128]{1,0:T(8,128)S(1)}, f32[4,8,112,128]{3,2,1,0:T(8,128)}, f32[4,8,112,128]{3,2,1,0:T(8,128)}, f32[4,8,112,128]{3,2,1,0:T(...) while((s32[]{:T(128)}, f32[112,128]{1,0:T(8,128)S(1)}, ...), condition=%wide.region_10.10_spmd.clone, body=%wide.region_9.9_spmd.clone.sunk | while | flops 817161 | bytes 4588343 | solution.py:85
  172.9 3.2 %fusion.132 = f32[33,112,128]{2,1,0:T(8,128)S(1)} fusion(f32[1,112,128]{2,1,0:T(8,128)S(1)} %slice_multiply_fusion.2, f32[1,112,128]{2,1,0:T(8,128)S(1)} %broadcast_in_dim.228, f32[32,112,128]{2,1,0:T(8,128)} %bitcast.684, f32[32,112,128]{2,1,0:T(8,128)} %bitcast.648, f32[32,112,128]{2,1,0:T(8,128)} %bitcast.650, f32[32,112,128]{2,1,0:T(8,128)S(1)} %copy-done.2, ...), kind=kLoop, calls=%fused_computation.180.clone.1 | loop fusion | flops 4257792 | bytes 9347584 | tf_op jit(solution)/shard_map/while/body/eval_jaxpr/sub | solution.py:97
  177.2 5.9 %fusion.127 = f32[32,112,128]{2,1,0:T(8,128)S(1)} fusion(f32[32,128,112,1]{1,2,3,0:T(8,128)S(1)} %fusion.126), kind=kOutput, calls=%fused_computation.191.clone.1 | output fusion | flops 14221312 | bytes 3670016 | tf_op jit(solution)/shard_map/while/body/eval_jaxpr/jit(cumsum)/reduce_window_sum | solution.py:25
  184.4 2.8 bitcast_multiply_fusion.5
  187.2 1.4 broadcast.891.clone
  188.6 1.4 broadcast.891.clone.1
  190.0 14.0 %while.86 = (s32[]{:T(128)}, f32[112,128]{1,0:T(8,128)S(1)}, f32[112,128]{1,0:T(8,128)S(1)}, f32[4,8,112,128]{3,2,1,0:T(8,128)}, f32[4,8,112,128]{3,2,1,0:T(8,12...) while((s32[]{:T(128)}, f32[112,128]{1,0:T(8,128)S(1)}, ...), condition=%wide.region_8.8_spmd, body=%wide.region_7.7_spmd.sunk | while | flops 1290248 | bytes 6136109 | solution.py:58
  190.0 1.4 bitcast_dynamic-update-slice_fusion.53
  193.5 1.4 bitcast_dynamic-update-slice_fusion.53
  197.0 1.4 bitcast_dynamic-update-slice_fusion.53
  200.5 1.4 bitcast_dynamic-update-slice_fusion.53
  204.0 3.5 %fusion.131 = f32[32,112,128]{2,1,0:T(8,128)} fusion(f32[1,112,128]{2,1,0:T(8,128)S(1)} %broadcast_in_dim.228, f32[32,112,128]{2,1,0:T(8,128)} %bitcast.650), kind=kLoop, calls=%fused_computation.184.clone.1 | loop fusion | flops 458752 | bytes 3727360 | tf_op jit(solution)/shard_map/while/body/eval_jaxpr/concatenate | solution.py:68
  208.3 2.9 %fusion.130 = f32[32,112,128]{2,1,0:T(8,128)} fusion(f32[1,112,128]{2,1,0:T(8,128)S(1)} %slice_multiply_fusion.2, f32[32,112,128]{2,1,0:T(8,128)} %bitcast.648), kind=kLoop, calls=%fused_computation.183.clone.1 | loop fusion | flops 458752 | bytes 3727360 | tf_op jit(solution)/shard_map/while/body/eval_jaxpr/concatenate | solution.py:69
  211.2 1.4 broadcast.891
  212.6 34.4 %while.87 = (s32[]{:T(128)}, f32[112,128]{1,0:T(8,128)S(1)}, f32[4,8,112,128]{3,2,1,0:T(8,128)}, f32[4,8,112,128]{3,2,1,0:T(8,128)}, f32[4,8,112,128]{3,2,1,0:T(...) while((s32[]{:T(128)}, f32[112,128]{1,0:T(8,128)S(1)}, ...), condition=%wide.region_10.10_spmd.clone, body=%wide.region_9.9_spmd.clone.sunk | while | flops 817161 | bytes 4588343 | solution.py:85
  247.0 3.2 %fusion.132 = f32[33,112,128]{2,1,0:T(8,128)S(1)} fusion(f32[1,112,128]{2,1,0:T(8,128)S(1)} %slice_multiply_fusion.2, f32[1,112,128]{2,1,0:T(8,128)S(1)} %broadcast_in_dim.228, f32[32,112,128]{2,1,0:T(8,128)} %bitcast.684, f32[32,112,128]{2,1,0:T(8,128)} %bitcast.648, f32[32,112,128]{2,1,0:T(8,128)} %bitcast.650, f32[32,112,128]{2,1,0:T(8,128)S(1)} %copy-done.2, ...), kind=kLoop, calls=%fused_computation.180.clone.1 | loop fusion | flops 4257792 | bytes 9347584 | tf_op jit(solution)/shard_map/while/body/eval_jaxpr/sub | solution.py:97
  251.6 4.2 %all-to-all-start.4 = ((f32[32,8,1,128]{3,0,2,1:T(8,128)}), f32[32,8,1,128]{3,0,2,1:T(8,128)S(1)}, u32[]{:S(2)}, u32[]{:S(2)}) async-start(f32[32,8,1,128]{3,0,2,1:T(8,128)} %bitcast_select_fusion.1), calls=%async_computation.4 | async-start | bytes 262144 | tf_op jit(solution)/shard_map/all_to_all | solution.py:187
  256.2 5.5 %all-to-all-done.4 = f32[32,8,1,128]{3,0,2,1:T(8,128)S(1)} async-done(((f32[32,8,1,128]{3,0,2,1:T(8,128)}), f32[32,8,1,128]{3,0,2,1:T(8,128)S(1)}, u32[]{:S(2)}, u32[]{:S(2)}) %all-to-all-start.4) | async-done | bytes 131104 | tf_op jit(solution)/shard_map/all_to_all | solution.py:187
  263.3 3.9 %all-to-all-start.5 = ((f32[32,1,512]{2,1,0:T(1,128)}), f32[32,1,512]{2,1,0:T(1,128)S(1)}, u32[]{:S(2)}, u32[]{:S(2)}) async-start(f32[32,1,512]{2,1,0:T(1,128)} %reshape.962), calls=%async_computation.5 | async-start | bytes 131072 | tf_op jit(solution)/shard_map/all_to_all | solution.py:195
  267.2 11.1 %all-to-all-done.5 = f32[32,1,512]{2,1,0:T(1,128)S(1)} async-done(((f32[32,1,512]{2,1,0:T(1,128)}), f32[32,1,512]{2,1,0:T(1,128)S(1)}, u32[]{:S(2)}, u32[]{:S(2)}) %all-to-all-start.5) | async-done | bytes 65568 | tf_op jit(solution)/shard_map/all_to_all | solution.py:195
  279.7 1.8 scatter_custom_fusion
  (333 shorter events, 114.0 us)
Async XLA Ops:
  5.5 39.7 %all-to-all-start = ((bf16[2,1,32,16]{3,0,1,2:T(2,128)(2,1)}), bf16[2,1,32,16]{3,0,1,2:T(2,128)(2,1)S(1)}, u32[]{:S(2)}, u32[]{:S(2)}) async-start(bf16[2,1,32,16]{3,0,1,2:T(2,128)(2,1)} %broadcast_select_fusion.1), calls=%async_computation | async-start | bytes 32768 | tf_op jit(solution)/shard_map/all_to_all | solution.py:140
  45.1 23.9 %all-to-all-start.2 = ((bf16[32,2,2304]{2,1,0:T(2,128)(2,1)}), bf16[32,2,2304]{2,1,0:T(2,128)(2,1)S(1)}, u32[]{:S(2)}, u32[]{:S(2)}) async-start(bf16[32,2,2304]{2,1,0:T(2,128)(2,1)} %reshape.960), calls=%async_computation.2 | async-start | bytes 589824 | tf_op jit(solution)/shard_map/all_to_all | solution.py:139
  69.0 12.5 %all-to-all-start.1 = ((bf16[2,1,8,1,128]{4,0,3,1,2:T(2,128)(2,1)}), bf16[2,1,8,1,128]{4,0,3,1,2:T(2,128)(2,1)S(1)}, u32[]{:S(2)}, u32[]{:S(2)}) async-start(bf16[2,1,8,1,128]{4,0,3,1,2:T(2,128)(2,1)} %fusion.84), calls=%async_computation.1 | async-start | bytes 8192 | tf_op jit(solution)/shard_map/all_to_all | solution.py:166
  78.6 23.6 %copy-start.4 = (bf16[112,60]{0,1:T(8,128)(2,1)S(1)}, bf16[112,60]{0,1:T(8,128)(2,1)}, u32[]{:S(2)}) copy-start(bf16[112,60]{0,1:T(8,128)(2,1)} %param.23) | copy-start | bytes 40324
  78.6 23.6 %copy-start.10 = (bf16[112,7,60]{0,2,1:T(8,128)(2,1)S(1)}, bf16[112,7,60]{0,2,1:T(8,128)(2,1)}, u32[]{:S(2)}) copy-start(bf16[112,7,60]{0,2,1:T(8,128)(2,1)} %param.22) | copy-start | bytes 282244
  81.5 19.9 %all-to-all-start.3 = ((bf16[9,32,8,1,128]{4,1,0,3,2:T(8,128)(2,1)}), bf16[9,32,8,1,128]{4,1,0,3,2:T(8,128)(2,1)S(1)}, u32[]{:S(2)}, u32[]{:S(2)}) async-start(bf16[9,32,8,1,128]{4,1,0,3,2:T(8,128)(2,1)} %fusion.81), calls=%async_computation.3 | async-start | bytes 1179648 | tf_op jit(solution)/shard_map/all_to_all | solution.py:165
  102.2 148.7 %copy-start.6 = (pred[8]{0:T(512)(128)(4,1)S(1)}, pred[8]{0:T(512)(128)(4,1)}, u32[]{:S(2)}) copy-start(pred[8]{0:T(512)(128)(4,1)} %get-tuple-element.492) | copy-start | bytes 28
  102.2 153.7 %copy-start.8 = (s32[4]{0:T(128)S(1)}, s32[4]{0:T(128)}, u32[]{:S(2)}) copy-start(s32[4]{0:T(128)} %param.21) | copy-start | bytes 52
  102.2 153.6 %copy-start.9 = (pred[4]{0:T(512)(128)(4,1)S(1)}, pred[4]{0:T(512)(128)(4,1)}, u32[]{:S(2)}) copy-start(pred[4]{0:T(512)(128)(4,1)} %get-tuple-element.489) | copy-start | bytes 16
  102.2 154.0 %copy-start.7 = (s32[4]{0:T(128)S(1)}, s32[4]{0:T(128)}, u32[]{:S(2)}) copy-start(s32[4]{0:T(128)} %get-tuple-element.490) | copy-start | bytes 52
  109.1 1.2 copy-start.1
  110.4 2.8 copy-start.3
  130.0 3.5 %copy-start = (f32[4,8,112,128]{3,2,1,0:T(8,128)}, f32[4,8,112,128]{3,2,1,0:T(8,128)S(1)}, u32[]{:S(2)}) copy-start(f32[4,8,112,128]{3,2,1,0:T(8,128)S(1)} %get-tuple-element.953) | copy-start | bytes 5505028 | tf_op jit(solution)/shard_map/while
  138.5 34.4 %copy-start.2 = (f32[32,112,128]{2,1,0:T(8,128)S(1)}, f32[32,112,128]{2,1,0:T(8,128)}, u32[]{:S(2)}) copy-start(f32[32,112,128]{2,1,0:T(8,128)} %copy-done.1) | copy-start | bytes 5505028 | tf_op jit(solution)/shard_map/while
  183.2 1.2 copy-start.1
  184.4 2.8 copy-start.3
  204.0 3.5 %copy-start = (f32[4,8,112,128]{3,2,1,0:T(8,128)}, f32[4,8,112,128]{3,2,1,0:T(8,128)S(1)}, u32[]{:S(2)}) copy-start(f32[4,8,112,128]{3,2,1,0:T(8,128)S(1)} %get-tuple-element.953) | copy-start | bytes 5505028 | tf_op jit(solution)/shard_map/while
  212.6 34.4 %copy-start.2 = (f32[32,112,128]{2,1,0:T(8,128)S(1)}, f32[32,112,128]{2,1,0:T(8,128)}, u32[]{:S(2)}) copy-start(f32[32,112,128]{2,1,0:T(8,128)} %copy-done.1) | copy-start | bytes 5505028 | tf_op jit(solution)/shard_map/while
  250.3 16.9 %copy-start.5 = (s32[512]{0:T(512)S(1)}, s32[512]{0:T(512)}, u32[]{:S(2)}) copy-start(s32[512]{0:T(512)} %param.20) | copy-start | bytes 6148
  251.6 10.1 %all-to-all-start.4 = ((f32[32,8,1,128]{3,0,2,1:T(8,128)}), f32[32,8,1,128]{3,0,2,1:T(8,128)S(1)}, u32[]{:S(2)}, u32[]{:S(2)}) async-start(f32[32,8,1,128]{3,0,2,1:T(8,128)} %bitcast_select_fusion.1), calls=%async_computation.4 | async-start | bytes 262144 | tf_op jit(solution)/shard_map/all_to_all | solution.py:187
  263.3 15.0 %all-to-all-start.5 = ((f32[32,1,512]{2,1,0:T(1,128)}), f32[32,1,512]{2,1,0:T(1,128)S(1)}, u32[]{:S(2)}, u32[]{:S(2)}) async-start(f32[32,1,512]{2,1,0:T(1,128)} %reshape.962), calls=%async_computation.5 | async-start | bytes 131072 | tf_op jit(solution)/shard_map/all_to_all | solution.py:195
where the time goes:
time: 288 us; the launch traced here: 282 us
  other arithmetic  125 us (43%)
  local copies, waits for them, and re-layouts  51.3 us (18%)
  starting transfers between devices  45.7 us (16%)
  waiting for transfers between devices  44 us (15%)
  matrix products  7 us (2%)
  blocking collectives  6.82 us (2%)
    while x74, other arithmetic  72.5 us
    all_to_all x1, waiting for transfers between devices, local(): lax.all_to_all(send_fields, 'band', split_axis=2, concat_axis=2, tiled=True)  15.1 us
    dynamic_update_slice x16, local copies, waits for them, and re-layouts, column_heating(): lax.scan(upward, (floor_refl, floor_source), (reflect.reshape(grouped_sha...  14.5 us
    all_to_all x1, starting transfers between devices, local(): lax.all_to_all(ground, 'span', split_axis=2, concat_axis=2, tiled=True)  14.5 us
    another operation x2, other arithmetic, column_heating(): column_path = jnp.cumsum(optical_depth, axis=0)  11.9 us
    all_to_all x1, starting transfers between devices, local(): lax.all_to_all(fields, 'span', split_axis=2, concat_axis=2, tiled=True)  11.3 us
    all_to_all x1, waiting for transfers between devices, local(): lax.all_to_all(physics_heat, 'span', split_axis=1, concat_axis=1, tiled=T...  11.1 us
    all_to_all x1, waiting for transfers between devices, local(): lax.all_to_all(fields, 'span', split_axis=2, concat_axis=2, tiled=True)  10.5 us
  transfers between devices with their start and end apart: 6, of which 5 were waited for; matrix products, arithmetic and copies ran while one was open for 8% of the time, Pallas kernels for 0%

commit v1 on v0

--- a/solution.py
+++ b/solution.py
@@ -162,7 +162,12 @@
     )
     send_ground = jnp.take(ground, chosen, axis=2).reshape(2, 1, band_count, slot_count, block_cols)
     got_fields, got_ground = (
-        lax.all_to_all(send_fields, "band", split_axis=2, concat_axis=2, tiled=True),
+        jnp.concatenate(
+            lax.all_to_all(
+                jnp.stack(jnp.split(send_fields, lax.axis_size("band"), axis=2)), "band", 0, 0
+            ),
+            axis=2,
+        ),
         lax.all_to_all(send_ground, "band", split_axis=2, concat_axis=2, tiled=True),
     )
     work_rank = jnp.arange(working, dtype=jnp.int32) * band_count + me_band

time: 288 us -> 291 us (1.010)
  local copies, waits for them, and re-layouts: 51.3 us -> 56.3 us
    unnamed x21 -> x28, local copies, waits for them, and re-layouts: 5.27 us -> 9.66 us
    all_to_all x1, starting transfers between devices: 14.5 us -> 11 us  [local(): lax.all_to_all(ground, 'span', split_axis=2, concat_axis=2, tiled=True)]
    another operation x6 -> x7, local copies, waits for them, and re-layouts: 8.43 us -> 8.97 us
  transfers between devices with their start and end apart: 6 -> 6, of which waited for: 5 -> 4; matrix products, arithmetic and copies ran while one was open for 8% -> 9% of each run, Pallas kernels for 0% -> 0%
where the time goes in v1:
time: 291 us; the launch traced here: 285 us
  other arithmetic  124 us (43%)
  local copies, waits for them, and re-layouts  56.3 us (19%)
  starting transfers between devices  43.8 us (15%)
  waiting for transfers between devices  42.1 us (14%)
  blocking collectives  9.46 us (3%)
  matrix products  7.01 us (2%)
    while x74, other arithmetic  72.5 us
    dynamic_update_slice x16, local copies, waits for them, and re-layouts, column_heating(): lax.scan(upward, (floor_refl, floor_source), (reflect.reshape(grouped_sha...  14.6 us
    all_to_all x1, waiting for transfers between devices, local(): lax.all_to_all(jnp.stack(jnp.split(send_fields, lax.axis_size('band'), ax...  14.4 us
    another operation x2, other arithmetic, column_heating(): column_path = jnp.cumsum(optical_depth, axis=0)  11.9 us
    all_to_all x1, starting transfers between devices, local(): lax.all_to_all(fields, 'span', split_axis=2, concat_axis=2, tiled=True)  11.6 us
    all_to_all x1, waiting for transfers between devices, local(): lax.all_to_all(fields, 'span', split_axis=2, concat_axis=2, tiled=True)  11.1 us
    all_to_all x1, waiting for transfers between devices, local(): lax.all_to_all(physics_heat, 'span', split_axis=1, concat_axis=1, tiled=T...  11.1 us
    all_to_all x1, starting transfers between devices, local(): lax.all_to_all(ground, 'span', split_axis=2, concat_axis=2, tiled=True)  11 us
  transfers between devices with their start and end apart: 6, of which 4 were waited for; matrix products, arithmetic and copies ran while one was open for 9% of the time, Pallas kernels for 0%

profile of v1, /device:TPU:1, one launch (start us, length us, event | category | flops | bytes accessed | tf_op | source)
XLA Modules:
  0.0 285.4 jit_solution(2632677584849667960)
XLA Ops:
  1.5 1.3 dynamic-slice
  4.3 9.5 %all-reduce.2 = s32[32]{0:T(128)S(1)} all-reduce(s32[32]{0:T(128)S(1)} %dynamic-update-slice), channel_id=1, replica_groups=mesh['band'=8,'span'=32] {'band'}, use_global_device_ids=true, to_apply=%add.2 | all-reduce | flops 32 | bytes 256
  16.0 1.3 gather_fusion.1
  18.3 11.0 %all-to-all-start = ((bf16[2,1,32,16]{3,0,1,2:T(2,128)(2,1)}), bf16[2,1,32,16]{3,0,1,2:T(2,128)(2,1)S(1)}, u32[]{:S(2)}, u32[]{:S(2)}) async-start(bf16[2,1,32,16]{3,0,1,2:T(2,128)(2,1)} %broadcast_select_fusion.1), calls=%async_computation | async-start | bytes 32768 | tf_op jit(solution)/shard_map/all_to_all | solution.py:140
  32.0 1.8 compare_and_fusion.4
  35.6 2.0 copy.102
  37.6 2.7 gather_fusion.4
  40.4 1.9 copy.103
  42.7 1.5 reshape.960
  44.2 11.6 %all-to-all-start.2 = ((bf16[32,2,2304]{2,1,0:T(2,128)(2,1)}), bf16[32,2,2304]{2,1,0:T(2,128)(2,1)S(1)}, u32[]{:S(2)}, u32[]{:S(2)}) async-start(bf16[32,2,2304]{2,1,0:T(2,128)(2,1)} %reshape.960), calls=%async_computation.2 | async-start | bytes 589824 | tf_op jit(solution)/shard_map/all_to_all | solution.py:139
  57.2 11.1 %all-to-all-done.2 = bf16[32,2,2304]{2,1,0:T(2,128)(2,1)S(1)} async-done(((bf16[32,2,2304]{2,1,0:T(2,128)(2,1)}), bf16[32,2,2304]{2,1,0:T(2,128)(2,1)S(1)}, u32[]{:S(2)}, u32[]{:S(2)}) %all-to-all-start.2) | async-done | bytes 294944 | tf_op jit(solution)/shard_map/all_to_all | solution.py:139
  68.4 8.0 %all-to-all-start.1 = ((bf16[2,1,8,1,128]{4,0,3,1,2:T(2,128)(2,1)}), bf16[2,1,8,1,128]{4,0,3,1,2:T(2,128)(2,1)S(1)}, u32[]{:S(2)}, u32[]{:S(2)}) async-start(bf16[2,1,8,1,128]{4,0,3,1,2:T(2,128)(2,1)} %fusion.91), calls=%async_computation.1 | async-start | bytes 8192 | tf_op jit(solution)/shard_map/all_to_all | solution.py:171
  83.7 5.1 %all-to-all-start.3 = ((bf16[8,9,32,1,1,128]{5,2,1,4,3,0:T(8,128)(2,1)}), bf16[8,9,32,1,1,128]{5,2,1,4,3,0:T(8,128)(2,1)S(1)}, u32[]{:S(2)}, u32[]{:S(2)}) async-start(bf16[8,9,32,1,1,128]{5,2,1,4,3,0:T(8,128)(2,1)} %fusion.83), calls=%async_computation.3 | async-start | bytes 1179648 | tf_op jit(solution)/shard_map/all_to_all | solution.py:166
  90.2 14.4 %all-to-all-done.3 = bf16[8,9,32,1,1,128]{5,2,1,4,3,0:T(8,128)(2,1)S(1)} async-done(((bf16[8,9,32,1,1,128]{5,2,1,4,3,0:T(8,128)(2,1)}), bf16[8,9,32,1,1,128]{5,2,1,4,3,0:T(8,128)(2,1)S(1)}, u32[]{:S(2)}, u32[]{:S(2)}) %all-to-all-start.3) | async-done | bytes 589856 | tf_op jit(solution)/shard_map/all_to_all | solution.py:166
  105.3 148.1 %while.85 = (s32[]{:T(128)}, f32[2,32,128]{2,1,0:T(8,128)S(1)}, bf16[2,2,1,128]{3,0,1,2:T(2,128)(2,1)S(1)}, bf16[2,9,32,128]{3,2,1,0:T(8,128)(2,1)S(1)}, bf16[11...) while((s32[]{:T(128)}, f32[2,32,128]{2,1,0:T(8,128)S(1)}, ...), condition=%wide.region_12.13_spmd, body=%wide.region_5.12_spmd.sunk | while | flops 469948672 | bytes 88375600 | solution.py:104
  106.3 5.9 %fusion.135 = f32[32,112,128]{2,1,0:T(8,128)S(1)} fusion(f32[32,128,112,1]{1,2,3,0:T(8,128)S(1)} %fusion.134), kind=kOutput, calls=%fused_computation.191.clone.1 | output fusion | flops 14221312 | bytes 3670016 | tf_op jit(solution)/shard_map/while/body/eval_jaxpr/jit(cumsum)/reduce_window_sum | solution.py:25
  113.4 2.8 bitcast_multiply_fusion.5
  116.2 1.4 broadcast.891.clone
  117.7 1.4 broadcast.891.clone.1
  119.0 14.0 %while.86 = (s32[]{:T(128)}, f32[112,128]{1,0:T(8,128)S(1)}, f32[112,128]{1,0:T(8,128)S(1)}, f32[4,8,112,128]{3,2,1,0:T(8,128)}, f32[4,8,112,128]{3,2,1,0:T(8,12...) while((s32[]{:T(128)}, f32[112,128]{1,0:T(8,128)S(1)}, ...), condition=%wide.region_8.8_spmd, body=%wide.region_7.7_spmd.sunk | while | flops 1290248 | bytes 6136109 | solution.py:58
  119.0 1.4 bitcast_dynamic-update-slice_fusion.53
  122.5 1.4 bitcast_dynamic-update-slice_fusion.53
  126.0 1.4 bitcast_dynamic-update-slice_fusion.53
  129.5 1.4 bitcast_dynamic-update-slice_fusion.53
  133.0 3.5 %fusion.139 = f32[32,112,128]{2,1,0:T(8,128)} fusion(f32[1,112,128]{2,1,0:T(8,128)S(1)} %broadcast_in_dim.232, f32[32,112,128]{2,1,0:T(8,128)} %bitcast.687), kind=kLoop, calls=%fused_computation.184.clone.1 | loop fusion | flops 458752 | bytes 3727360 | tf_op jit(solution)/shard_map/while/body/eval_jaxpr/concatenate | solution.py:68
  137.3 2.9 %fusion.138 = f32[32,112,128]{2,1,0:T(8,128)} fusion(f32[1,112,128]{2,1,0:T(8,128)S(1)} %slice_multiply_fusion.2, f32[32,112,128]{2,1,0:T(8,128)} %bitcast.685), kind=kLoop, calls=%fused_computation.183.clone.1 | loop fusion | flops 458752 | bytes 3727360 | tf_op jit(solution)/shard_map/while/body/eval_jaxpr/concatenate | solution.py:69
  140.2 1.4 broadcast.891
  141.6 34.4 %while.87 = (s32[]{:T(128)}, f32[112,128]{1,0:T(8,128)S(1)}, f32[4,8,112,128]{3,2,1,0:T(8,128)}, f32[4,8,112,128]{3,2,1,0:T(8,128)}, f32[4,8,112,128]{3,2,1,0:T(...) while((s32[]{:T(128)}, f32[112,128]{1,0:T(8,128)S(1)}, ...), condition=%wide.region_10.10_spmd.clone, body=%wide.region_9.9_spmd.clone.sunk | while | flops 817161 | bytes 4588343 | solution.py:85
  176.0 3.2 %fusion.140 = f32[33,112,128]{2,1,0:T(8,128)S(1)} fusion(f32[1,112,128]{2,1,0:T(8,128)S(1)} %slice_multiply_fusion.2, f32[1,112,128]{2,1,0:T(8,128)S(1)} %broadcast_in_dim.232, f32[32,112,128]{2,1,0:T(8,128)} %bitcast.721, f32[32,112,128]{2,1,0:T(8,128)} %bitcast.685, f32[32,112,128]{2,1,0:T(8,128)} %bitcast.687, f32[32,112,128]{2,1,0:T(8,128)S(1)} %copy-done.2, ...), kind=kLoop, calls=%fused_computation.180.clone.1 | loop fusion | flops 4257792 | bytes 9347584 | tf_op jit(solution)/shard_map/while/body/eval_jaxpr/sub | solution.py:97
  180.3 5.9 %fusion.135 = f32[32,112,128]{2,1,0:T(8,128)S(1)} fusion(f32[32,128,112,1]{1,2,3,0:T(8,128)S(1)} %fusion.134), kind=kOutput, calls=%fused_computation.191.clone.1 | output fusion | flops 14221312 | bytes 3670016 | tf_op jit(solution)/shard_map/while/body/eval_jaxpr/jit(cumsum)/reduce_window_sum | solution.py:25
  187.5 2.8 bitcast_multiply_fusion.5
  190.3 1.4 broadcast.891.clone
  191.7 1.4 broadcast.891.clone.1
  193.1 14.0 %while.86 = (s32[]{:T(128)}, f32[112,128]{1,0:T(8,128)S(1)}, f32[112,128]{1,0:T(8,128)S(1)}, f32[4,8,112,128]{3,2,1,0:T(8,128)}, f32[4,8,112,128]{3,2,1,0:T(8,12...) while((s32[]{:T(128)}, f32[112,128]{1,0:T(8,128)S(1)}, ...), condition=%wide.region_8.8_spmd, body=%wide.region_7.7_spmd.sunk | while | flops 1290248 | bytes 6136109 | solution.py:58
  193.1 1.4 bitcast_dynamic-update-slice_fusion.53
  196.6 1.4 bitcast_dynamic-update-slice_fusion.53
  200.1 1.4 bitcast_dynamic-update-slice_fusion.53
  203.6 1.4 bitcast_dynamic-update-slice_fusion.53
  207.1 3.5 %fusion.139 = f32[32,112,128]{2,1,0:T(8,128)} fusion(f32[1,112,128]{2,1,0:T(8,128)S(1)} %broadcast_in_dim.232, f32[32,112,128]{2,1,0:T(8,128)} %bitcast.687), kind=kLoop, calls=%fused_computation.184.clone.1 | loop fusion | flops 458752 | bytes 3727360 | tf_op jit(solution)/shard_map/while/body/eval_jaxpr/concatenate | solution.py:68
  211.4 2.9 %fusion.138 = f32[32,112,128]{2,1,0:T(8,128)} fusion(f32[1,112,128]{2,1,0:T(8,128)S(1)} %slice_multiply_fusion.2, f32[32,112,128]{2,1,0:T(8,128)} %bitcast.685), kind=kLoop, calls=%fused_computation.183.clone.1 | loop fusion | flops 458752 | bytes 3727360 | tf_op jit(solution)/shard_map/while/body/eval_jaxpr/concatenate | solution.py:69
  214.3 1.4 broadcast.891
  215.6 34.4 %while.87 = (s32[]{:T(128)}, f32[112,128]{1,0:T(8,128)S(1)}, f32[4,8,112,128]{3,2,1,0:T(8,128)}, f32[4,8,112,128]{3,2,1,0:T(8,128)}, f32[4,8,112,128]{3,2,1,0:T(...) while((s32[]{:T(128)}, f32[112,128]{1,0:T(8,128)S(1)}, ...), condition=%wide.region_10.10_spmd.clone, body=%wide.region_9.9_spmd.clone.sunk | while | flops 817161 | bytes 4588343 | solution.py:85
  250.1 3.2 %fusion.140 = f32[33,112,128]{2,1,0:T(8,128)S(1)} fusion(f32[1,112,128]{2,1,0:T(8,128)S(1)} %slice_multiply_fusion.2, f32[1,112,128]{2,1,0:T(8,128)S(1)} %broadcast_in_dim.232, f32[32,112,128]{2,1,0:T(8,128)} %bitcast.721, f32[32,112,128]{2,1,0:T(8,128)} %bitcast.685, f32[32,112,128]{2,1,0:T(8,128)} %bitcast.687, f32[32,112,128]{2,1,0:T(8,128)S(1)} %copy-done.2, ...), kind=kLoop, calls=%fused_computation.180.clone.1 | loop fusion | flops 4257792 | bytes 9347584 | tf_op jit(solution)/shard_map/while/body/eval_jaxpr/sub | solution.py:97
  254.7 4.2 %all-to-all-start.4 = ((f32[32,8,1,128]{3,0,2,1:T(8,128)}), f32[32,8,1,128]{3,0,2,1:T(8,128)S(1)}, u32[]{:S(2)}, u32[]{:S(2)}) async-start(f32[32,8,1,128]{3,0,2,1:T(8,128)} %bitcast_select_fusion.1), calls=%async_computation.4 | async-start | bytes 262144 | tf_op jit(solution)/shard_map/all_to_all | solution.py:192
  259.3 5.5 %all-to-all-done.4 = f32[32,8,1,128]{3,0,2,1:T(8,128)S(1)} async-done(((f32[32,8,1,128]{3,0,2,1:T(8,128)}), f32[32,8,1,128]{3,0,2,1:T(8,128)S(1)}, u32[]{:S(2)}, u32[]{:S(2)}) %all-to-all-start.4) | async-done | bytes 131104 | tf_op jit(solution)/shard_map/all_to_all | solution.py:192
  266.4 3.9 %all-to-all-start.5 = ((f32[32,1,512]{2,1,0:T(1,128)}), f32[32,1,512]{2,1,0:T(1,128)S(1)}, u32[]{:S(2)}, u32[]{:S(2)}) async-start(f32[32,1,512]{2,1,0:T(1,128)} %reshape.962), calls=%async_computation.5 | async-start | bytes 131072 | tf_op jit(solution)/shard_map/all_to_all | solution.py:200
  270.3 11.1 %all-to-all-done.5 = f32[32,1,512]{2,1,0:T(1,128)S(1)} async-done(((f32[32,1,512]{2,1,0:T(1,128)}), f32[32,1,512]{2,1,0:T(1,128)S(1)}, u32[]{:S(2)}, u32[]{:S(2)}) %all-to-all-start.5) | async-done | bytes 65568 | tf_op jit(solution)/shard_map/all_to_all | solution.py:200
  282.9 1.8 scatter_custom_fusion
  (339 shorter events, 117.0 us)
Async XLA Ops:
  18.3 25.9 %all-to-all-start = ((bf16[2,1,32,16]{3,0,1,2:T(2,128)(2,1)}), bf16[2,1,32,16]{3,0,1,2:T(2,128)(2,1)S(1)}, u32[]{:S(2)}, u32[]{:S(2)}) async-start(bf16[2,1,32,16]{3,0,1,2:T(2,128)(2,1)} %broadcast_select_fusion.1), calls=%async_computation | async-start | bytes 32768 | tf_op jit(solution)/shard_map/all_to_all | solution.py:140
  44.2 24.2 %all-to-all-start.2 = ((bf16[32,2,2304]{2,1,0:T(2,128)(2,1)}), bf16[32,2,2304]{2,1,0:T(2,128)(2,1)S(1)}, u32[]{:S(2)}, u32[]{:S(2)}) async-start(bf16[32,2,2304]{2,1,0:T(2,128)(2,1)} %reshape.960), calls=%async_computation.2 | async-start | bytes 589824 | tf_op jit(solution)/shard_map/all_to_all | solution.py:139
  68.4 15.3 %all-to-all-start.1 = ((bf16[2,1,8,1,128]{4,0,3,1,2:T(2,128)(2,1)}), bf16[2,1,8,1,128]{4,0,3,1,2:T(2,128)(2,1)S(1)}, u32[]{:S(2)}, u32[]{:S(2)}) async-start(bf16[2,1,8,1,128]{4,0,3,1,2:T(2,128)(2,1)} %fusion.91), calls=%async_computation.1 | async-start | bytes 8192 | tf_op jit(solution)/shard_map/all_to_all | solution.py:171
  78.6 26.7 %copy-start.4 = (bf16[112,60]{0,1:T(8,128)(2,1)S(1)}, bf16[112,60]{0,1:T(8,128)(2,1)}, u32[]{:S(2)}) copy-start(bf16[112,60]{0,1:T(8,128)(2,1)} %param.23) | copy-start | bytes 40324
  78.6 26.7 %copy-start.10 = (bf16[112,7,60]{0,2,1:T(8,128)(2,1)S(1)}, bf16[112,7,60]{0,2,1:T(8,128)(2,1)}, u32[]{:S(2)}) copy-start(bf16[112,7,60]{0,2,1:T(8,128)(2,1)} %param.22) | copy-start | bytes 282244
  83.7 20.9 %all-to-all-start.3 = ((bf16[8,9,32,1,1,128]{5,2,1,4,3,0:T(8,128)(2,1)}), bf16[8,9,32,1,1,128]{5,2,1,4,3,0:T(8,128)(2,1)S(1)}, u32[]{:S(2)}, u32[]{:S(2)}) async-start(bf16[8,9,32,1,1,128]{5,2,1,4,3,0:T(8,128)(2,1)} %fusion.83), calls=%async_computation.3 | async-start | bytes 1179648 | tf_op jit(solution)/shard_map/all_to_all | solution.py:166
  105.3 148.7 %copy-start.6 = (pred[8]{0:T(512)(128)(4,1)S(1)}, pred[8]{0:T(512)(128)(4,1)}, u32[]{:S(2)}) copy-start(pred[8]{0:T(512)(128)(4,1)} %get-tuple-element.492) | copy-start | bytes 28
  105.3 153.7 %copy-start.8 = (s32[4]{0:T(128)S(1)}, s32[4]{0:T(128)}, u32[]{:S(2)}) copy-start(s32[4]{0:T(128)} %param.21) | copy-start | bytes 52
  105.3 153.7 %copy-start.9 = (pred[4]{0:T(512)(128)(4,1)S(1)}, pred[4]{0:T(512)(128)(4,1)}, u32[]{:S(2)}) copy-start(pred[4]{0:T(512)(128)(4,1)} %get-tuple-element.489) | copy-start | bytes 16
  105.3 154.0 %copy-start.7 = (s32[4]{0:T(128)S(1)}, s32[4]{0:T(128)}, u32[]{:S(2)}) copy-start(s32[4]{0:T(128)} %get-tuple-element.490) | copy-start | bytes 52
  112.2 1.2 copy-start.1
  113.4 2.8 copy-start.3
  133.0 3.5 %copy-start = (f32[4,8,112,128]{3,2,1,0:T(8,128)}, f32[4,8,112,128]{3,2,1,0:T(8,128)S(1)}, u32[]{:S(2)}) copy-start(f32[4,8,112,128]{3,2,1,0:T(8,128)S(1)} %get-tuple-element.957) | copy-start | bytes 5505028 | tf_op jit(solution)/shard_map/while
  141.6 34.4 %copy-start.2 = (f32[32,112,128]{2,1,0:T(8,128)S(1)}, f32[32,112,128]{2,1,0:T(8,128)}, u32[]{:S(2)}) copy-start(f32[32,112,128]{2,1,0:T(8,128)} %copy-done.1) | copy-start | bytes 5505028 | tf_op jit(solution)/shard_map/while
  186.3 1.2 copy-start.1
  187.5 2.8 copy-start.3
  207.0 3.5 %copy-start = (f32[4,8,112,128]{3,2,1,0:T(8,128)}, f32[4,8,112,128]{3,2,1,0:T(8,128)S(1)}, u32[]{:S(2)}) copy-start(f32[4,8,112,128]{3,2,1,0:T(8,128)S(1)} %get-tuple-element.957) | copy-start | bytes 5505028 | tf_op jit(solution)/shard_map/while
  215.6 34.4 %copy-start.2 = (f32[32,112,128]{2,1,0:T(8,128)S(1)}, f32[32,112,128]{2,1,0:T(8,128)}, u32[]{:S(2)}) copy-start(f32[32,112,128]{2,1,0:T(8,128)} %copy-done.1) | copy-start | bytes 5505028 | tf_op jit(solution)/shard_map/while
  253.4 16.9 %copy-start.5 = (s32[512]{0:T(512)S(1)}, s32[512]{0:T(512)}, u32[]{:S(2)}) copy-start(s32[512]{0:T(512)} %param.20) | copy-start | bytes 6148
  254.7 10.1 %all-to-all-start.4 = ((f32[32,8,1,128]{3,0,2,1:T(8,128)}), f32[32,8,1,128]{3,0,2,1:T(8,128)S(1)}, u32[]{:S(2)}, u32[]{:S(2)}) async-start(f32[32,8,1,128]{3,0,2,1:T(8,128)} %bitcast_select_fusion.1), calls=%async_computation.4 | async-start | bytes 262144 | tf_op jit(solution)/shard_map/all_to_all | solution.py:192
  266.4 15.0 %all-to-all-start.5 = ((f32[32,1,512]{2,1,0:T(1,128)}), f32[32,1,512]{2,1,0:T(1,128)S(1)}, u32[]{:S(2)}, u32[]{:S(2)}) async-start(f32[32,1,512]{2,1,0:T(1,128)} %reshape.962), calls=%async_computation.5 | async-start | bytes 131072 | tf_op jit(solution)/shard_map/all_to_all | solution.py:200
